TPU v7x, 32 devices: a whole 2x2x4 slice. The times are simulated.
32 devices in a mesh: dp: 8 (over y, x, core), tensor: 4 (over z).
Axes of the slice: x: 2, y: 2, z: 4, core: 2. Of those that a mesh axis runs over, the one named last changes fastest.
Arguments:
- tokens: bfloat16 [8192, 1024], P(('dp', 'tensor')), may hold values from -6 to 6
- gain_attn: bfloat16 [1024], replicated, may hold values from 0.5 to 1.5
- w_query: bfloat16 [1024, 1024], P(None, 'tensor'), may hold values from -0.1875 to 0.1875
- w_key: bfloat16 [1024, 1024], P(None, 'tensor'), may hold values from -0.1875 to 0.1875
- w_value: bfloat16 [1024, 1024], P(None, 'tensor'), may hold values from -0.1875 to 0.1875
- w_out: bfloat16 [1024, 1024], P('tensor'), may hold values from -1 to 1
- gain_mlp: bfloat16 [1024], replicated, may hold values from 0.5 to 1.5
- w_gate: bfloat16 [1024, 2752], P(None, 'tensor'), may hold values from -0.1875 to 0.1875
- w_up: bfloat16 [1024, 2752], P(None, 'tensor'), may hold values from -0.1875 to 0.1875
- w_down: bfloat16 [2752, 1024], P('tensor'), may hold values from -0.21875 to 0.21875
- out_grad: bfloat16 [8192, 1024], P(('dp', 'tensor')), may hold values from -6 to 6
Outputs:
- output: bfloat16 [8192, 1024], P(('dp', 'tensor'))
- input_grad: float32 [8192, 1024], P(('dp', 'tensor'))
- grad_gain_attn: float32 [1024], replicated
- grad_query: float32 [1024, 1024], P(None, 'tensor')
- grad_key: float32 [1024, 1024], P(None, 'tensor')
- grad_value: float32 [1024, 1024], P(None, 'tensor')
- grad_out: float32 [1024, 1024], P('tensor')
- grad_gain_mlp: float32 [1024], replicated
- grad_gate: float32 [1024, 2752], P(None, 'tensor')
- grad_up: float32 [1024, 2752], P(None, 'tensor')
- grad_down: float32 [2752, 1024], P('tensor')
All inputs are finite; a program needn't handle non-finite values.
Results may differ from a plain program's by a relative error of at most 0.017.
Values may be sent and summed in bfloat16 or wider, within the bound.
No kernel may reach another device: no remote copies, remote signals or barrier semaphores. Data moves between devices by JAX's collectives and lax.ppermute only.
A program may use at most 128 MiB of HBM per device.

v0:
```python
import jax
import jax.numpy as jnp
from jax import lax
from jax.sharding import PartitionSpec as P

HEAD_DIM = 64
WINDOW = 64
SEQ_LEN = 1024


norm_eps = 1e-05
very_low = -1e30


def rms_norm(values, gain):
    return values * lax.rsqrt(jnp.mean(values * values, axis=-1, keepdims=True) + norm_eps) * gain


def mat_left(left, right):
    return lax.dot_general(
        left, right, (((0,), (0,)), ((), ())), preferred_element_type=jnp.float32
    )


def mat_right(left, right):
    return lax.dot_general(
        left, right, (((1,), (1,)), ((), ())), preferred_element_type=jnp.float32
    )


def band_mask(blocks, width):
    query_pos = jnp.arange(width)[:, None]
    key_pos = jnp.arange(2 * width)[None, :]
    banded = (key_pos >= query_pos + 1) & (key_pos <= query_pos + width)
    first_ok = jnp.arange(blocks)[:, None, None] > 0
    return banded[None] & ((key_pos >= width)[None] | first_ok)


def to_blocks(flat):
    return flat.reshape(
        flat.shape[0] // SEQ_LEN, SEQ_LEN // WINDOW, WINDOW, flat.shape[1] // HEAD_DIM, HEAD_DIM
    )


def with_previous(blocked):
    earlier = jnp.concatenate([jnp.zeros_like(blocked[:, :1]), blocked[:, :-1]], axis=1)
    return jnp.concatenate([earlier, blocked], axis=2)


def fold_previous(wide):
    width = wide.shape[2] // 2
    later = jnp.concatenate([wide[:, 1:, :width], jnp.zeros_like(wide[:, :1, :width])], axis=1)
    return wide[:, :, width:] + later


def band_scores(q_blocks, k_wide):
    scores = jnp.einsum(
        "snqhd,snkhd->snhqk", q_blocks, k_wide, preferred_element_type=jnp.float32
    ) * HEAD_DIM ** (-0.5)
    mask = band_mask(q_blocks.shape[1], WINDOW)[None, :, None]
    return (jnp.where(mask, scores, very_low), mask)


def attend_forward(queries, keys_all, values_all):
    q_blocks = to_blocks(queries)
    k_wide = with_previous(to_blocks(keys_all))
    v_wide = with_previous(to_blocks(values_all))
    scores, mask = band_scores(q_blocks, k_wide)
    top_score = jnp.max(scores, axis=-1, keepdims=True)
    expo = jnp.exp(scores - top_score)
    total = jnp.sum(expo, axis=-1, keepdims=True)
    probs = (expo / total).astype(jnp.bfloat16)
    log_sum = top_score + jnp.log(total)
    mixed = jnp.einsum("snhqk,snkhd->snqhd", probs, v_wide, preferred_element_type=jnp.float32)
    return (mixed.astype(jnp.bfloat16).reshape(queries.shape), log_sum)


def attend_backward(queries, keys_all, values_all, log_sum, mixed_grad):
    q_blocks = to_blocks(queries)
    k_wide = with_previous(to_blocks(keys_all))
    v_wide = with_previous(to_blocks(values_all))
    g_blocks = to_blocks(mixed_grad)
    scores, mask = band_scores(q_blocks, k_wide)
    probs = jnp.where(mask, jnp.exp(scores - log_sum), 0.0)
    prob_grad = jnp.einsum(
        "snqhd,snkhd->snhqk", g_blocks, v_wide, preferred_element_type=jnp.float32
    )
    inner_sum = jnp.sum(probs * prob_grad, axis=-1, keepdims=True)
    score_grad = (probs * (prob_grad - inner_sum)).astype(jnp.bfloat16)
    factor = HEAD_DIM ** (-0.5)
    query_grad = (
        jnp.einsum("snhqk,snkhd->snqhd", score_grad, k_wide, preferred_element_type=jnp.float32)
        * factor
    )
    key_wide = (
        jnp.einsum("snhqk,snqhd->snkhd", score_grad, q_blocks, preferred_element_type=jnp.float32)
        * factor
    )
    value_wide = jnp.einsum(
        "snhqk,snqhd->snkhd",
        probs.astype(jnp.bfloat16),
        g_blocks,
        preferred_element_type=jnp.float32,
    )
    query_grad = query_grad.astype(jnp.bfloat16).reshape(queries.shape)
    key_grad = fold_previous(key_wide).astype(jnp.bfloat16).reshape(queries.shape)
    value_grad = fold_previous(value_wide).astype(jnp.bfloat16).reshape(queries.shape)
    return (query_grad, key_grad, value_grad)


def local(
    tokens, gain_attn, w_query, w_key, w_value, w_out, gain_mlp, w_gate, w_up, w_down, out_grad
):
    token_float = tokens.astype(jnp.float32)
    attn_gain = gain_attn.astype(jnp.float32)
    mlp_gain = gain_mlp.astype(jnp.float32)
    normed_low = rms_norm(token_float, attn_gain).astype(jnp.bfloat16)
    normed_all = lax.all_gather(normed_low, "tensor", axis=0, tiled=True)
    queries = jnp.dot(normed_all, w_query, preferred_element_type=jnp.float32).astype(jnp.bfloat16)
    keys_all = jnp.dot(normed_all, w_key, preferred_element_type=jnp.float32).astype(jnp.bfloat16)
    values_all = jnp.dot(normed_all, w_value, preferred_element_type=jnp.float32).astype(
        jnp.bfloat16
    )
    attended, log_sum = attend_forward(queries, keys_all, values_all)
    piece = attended
    branch = lax.psum_scatter(
        jnp.dot(piece, w_out, preferred_element_type=jnp.float32),
        "tensor",
        scatter_dimension=0,
        tiled=True,
    )
    middle = token_float + branch
    normed_mid = rms_norm(middle, mlp_gain).astype(jnp.bfloat16)
    mid_all = lax.all_gather(normed_mid, "tensor", axis=0, tiled=True)
    gate_pre = jnp.dot(mid_all, w_gate, preferred_element_type=jnp.float32)
    up_pre = jnp.dot(mid_all, w_up, preferred_element_type=jnp.float32)
    gate_sig = jax.nn.sigmoid(gate_pre)
    silu_val = gate_pre * gate_sig
    hidden = (silu_val * up_pre).astype(jnp.bfloat16)
    piece = hidden
    mlp_out = lax.psum_scatter(
        jnp.dot(piece, w_down, preferred_element_type=jnp.float32).astype(jnp.bfloat16),
        "tensor",
        scatter_dimension=0,
        tiled=True,
    ).astype(jnp.float32)
    output = (middle + mlp_out).astype(jnp.bfloat16)
    grad_all = lax.all_gather(out_grad, "tensor", axis=0, tiled=True)
    grad_down = mat_left(hidden, grad_all)
    hidden_grad = mat_right(grad_all, w_down)
    up_grad = (hidden_grad * silu_val).astype(jnp.bfloat16)
    gate_grad = (hidden_grad * up_pre * gate_sig * (1.0 + gate_pre * (1.0 - gate_sig))).astype(
        jnp.bfloat16
    )
    grad_gate = mat_left(mid_all, gate_grad)
    grad_up = mat_left(mid_all, up_grad)
    grad_gate, grad_up, grad_down = lax.psum((grad_gate, grad_up, grad_down), "dp")
    mid_grad = lax.psum_scatter(
        mat_right(gate_grad, w_gate) + mat_right(up_grad, w_up),
        "tensor",
        scatter_dimension=0,
        tiled=True,
    )
    mid_pull = jax.vjp(rms_norm, middle, mlp_gain)[1]
    middle_norm_grad, mlp_gain_part = mid_pull(mid_grad)
    middle_grad = middle_norm_grad + out_grad.astype(jnp.float32)
    branch_all = lax.all_gather(middle_grad.astype(jnp.bfloat16), "tensor", axis=0, tiled=True)
    grad_out = mat_left(attended, branch_all)
    attended_grad = mat_right(branch_all, w_out).astype(jnp.bfloat16)
    query_grad, key_grad, value_grad = attend_backward(
        queries, keys_all, values_all, log_sum, attended_grad
    )
    grad_query = mat_left(normed_all, query_grad)
    grad_key = mat_left(normed_all, key_grad)
    grad_value = mat_left(normed_all, value_grad)
    normed_grad = lax.psum_scatter(
        (
            mat_right(query_grad, w_query)
            + mat_right(key_grad, w_key)
            + mat_right(value_grad, w_value)
        ).astype(jnp.bfloat16),
        "tensor",
        scatter_dimension=0,
        tiled=True,
    ).astype(jnp.float32)
    token_pull = jax.vjp(rms_norm, token_float, attn_gain)[1]
    token_norm_grad, attn_gain_part = token_pull(normed_grad)
    input_grad = middle_grad + token_norm_grad
    gain_totals = lax.psum((attn_gain_part, mlp_gain_part), ("dp", "tensor"))
    grad_query, grad_key, grad_value, grad_out = lax.psum(
        (grad_query, grad_key, grad_value, grad_out), "dp"
    )
    return (
        output,
        input_grad,
        gain_totals[0],
        grad_query,
        grad_key,
        grad_value,
        grad_out,
        gain_totals[1],
        grad_gate,
        grad_up,
        grad_down,
    )


def solution(mesh):
    return jax.shard_map(
        local,
        mesh=mesh,
        in_specs=(
            P(("dp", "tensor"), None),
            P(),
            P(None, "tensor"),
            P(None, "tensor"),
            P(None, "tensor"),
            P("tensor", None),
            P(),
            P(None, "tensor"),
            P(None, "tensor"),
            P("tensor", None),
            P(("dp", "tensor"), None),
        ),
        out_specs=(
            P(("dp", "tensor"), None),
            P(("dp", "tensor"), None),
            P(),
            P(None, "tensor"),
            P(None, "tensor"),
            P(None, "tensor"),
            P("tensor", None),
            P(),
            P(None, "tensor"),
            P(None, "tensor"),
            P("tensor", None),
        ),
        check_vma=False,
    )
```

profile of v0, /device:TPU:0, one launch (start us, length us, event | category | flops | bytes accessed | tf_op | source)
XLA Modules:
  0.0 746.2 jit_solution(10157777546044405719)
XLA Ops:
  12.4 47.8 %all-gather.5.cloned.1.call-done = bf16[1024,1024]{1,0:T(8,128)(2,1)} async-done(((bf16[256,1024]{1,0:T(8,128)(2,1)}), bf16[1024,1024]{1,0:T(8,128)(2,1)}) %all-gather.5.cloned.1.call-update) | async-done | bytes 2097168 | tf_op jit(solution)/shard_map/all_gather | solution.py:118
  60.2 3.1 convolution_convert_fusion.3
  63.3 2.9 reshape.264
  68.5 2.5 convolution_convert_fusion.4
  71.0 2.8 reshape.263
  76.0 2.5 convolution_convert_fusion.5
  78.6 2.8 reshape.261
  94.3 2.6 reshape.266
  96.9 3.9 fusion.37
  101.5 75.0 %reduce-scatter.5.cloned.1.call-done = f32[256,1024]{1,0:T(8,128)} async-done(((f32[1024,1024]{1,0:T(8,128)}), f32[256,1024]{1,0:T(8,128)}) %reduce-scatter.5.cloned.1.call-update) | async-done | bytes 1048592 | tf_op jit(solution)/shard_map/reduce_scatter | solution.py:126
  180.8 45.8 %all-gather.7.cloned.1.call-done = bf16[1024,1024]{1,0:T(8,128)(2,1)} async-done(((bf16[256,1024]{1,0:T(8,128)(2,1)}), bf16[1024,1024]{1,0:T(8,128)(2,1)}) %all-gather.7.cloned.1.call-update) | async-done | bytes 2097168 | tf_op jit(solution)/shard_map/all_gather | solution.py:134
  226.6 5.3 fusion.39
  232.0 3.2 fusion.38
  235.2 37.6 %all-gather.9.cloned.1.call-done = bf16[1024,1024]{1,0:T(8,128)(2,1)} async-done(((bf16[256,1024]{1,0:T(8,128)(2,1)}), bf16[1024,1024]{1,0:T(8,128)(2,1)}) %all-gather.9.cloned.1.call-update) | async-done | bytes 2097168 | tf_op jit(solution)/shard_map/all_gather | solution.py:148
  272.8 6.1 multiply_convert_fusion
  281.3 3.8 convolution_add_fusion
  285.2 75.6 %reduce-scatter.9.cloned.1.call-done = f32[256,1024]{1,0:T(8,128)} async-done(((f32[1024,1024]{1,0:T(8,128)}), f32[256,1024]{1,0:T(8,128)}) %reduce-scatter.9.cloned.1.call-update) | async-done | bytes 1048592 | tf_op jit(solution)/shard_map/reduce_scatter | solution.py:158
  366.3 45.8 %all-gather.11.cloned.1.call-done = bf16[1024,1024]{1,0:T(8,128)(2,1)} async-done(((bf16[256,1024]{1,0:T(8,128)(2,1)}), bf16[1024,1024]{1,0:T(8,128)(2,1)}) %all-gather.11.cloned.1.call-update) | async-done | bytes 2097168 | tf_op jit(solution)/shard_map/all_gather | solution.py:167
  412.1 3.2 convolution_convert_fusion.2
  415.3 2.9 reshape.267
  420.5 4.5 multiply_reduce_fusion
  433.2 2.6 reshape.268
  440.2 2.6 reshape.269
  447.2 2.8 reshape.270
  455.5 4.6 convolution_convert_fusion
  460.2 5.4 fusion.47
  465.6 3.2 fusion.49
  468.8 3.2 fusion.48
  479.0 19.2 %reduce-scatter.11.cloned.1.call-done = bf16[256,1024]{1,0:T(8,128)(2,1)} async-done(((bf16[1024,1024]{1,0:T(8,128)(2,1)}), bf16[256,1024]{1,0:T(8,128)(2,1)}) %reduce-scatter.11.cloned.1.call-update) | async-done | bytes 524304 | tf_op jit(solution)/shard_map/reduce_scatter | solution.py:176
  499.7 42.7 %all-reduce.4 = (f32[1024]{0:T(1024)}, f32[1024]{0:T(1024)}) all-reduce(f32[1024]{0:T(1024)S(1)} %get-tuple-element.13, f32[1024]{0:T(1024)S(1)} %get-tuple-element.11), channel_id=1, replica_groups=mesh['dp'=8,'tensor'=4] {'dp','tensor'}, use_global_device_ids=true, to_apply=%region_12.13 | all-reduce | flops 2048 | bytes 16384 | tf_op jit(solution)/shard_map/psum | solution.py:189
  544.9 3.2 fusion.15
  548.1 177.9 %all-reduce.8.cloned.1.call-done = (f32[1024,256]{1,0:T(8,128)}, f32[1024,256]{1,0:T(8,128)}, f32[1024,256]{1,0:T(8,128)}, f32[256,1024]{1,0:T(8,128)}, f32[1024...) async-done(((f32[1024,256]{1,0:T(8,128)}, f32[1024,256]{1,0:T(8,128)}, f32[1024,256]{1,0:T(8,128)}, f32[256,1024]{1,0:T(8,128)}, f32[1024,688]{0,1:T(8,128)}, ...) | async-done | bytes 12648464 | tf_op jit(solution)/shard_map/psum | solution.py:190
  (189 shorter events, 84.2 us)
Async XLA Ops:
  7.2 265.6 %copy-start = (bf16[688,1024]{1,0:T(8,128)(2,1)S(1)}, bf16[688,1024]{1,0:T(8,128)(2,1)}, u32[]{:S(2)}) copy-start(bf16[688,1024]{1,0:T(8,128)(2,1)} %param.20) | copy-start | bytes 4227076
  7.2 53.0 %copy-start.36 = (bf16[1024,256]{1,0:T(8,128)(2,1)S(1)}, bf16[1024,256]{1,0:T(8,128)(2,1)}, u32[]{:S(2)}) copy-start(bf16[1024,256]{1,0:T(8,128)(2,1)} %param.14) | copy-start | bytes 1572868
  7.2 53.0 %all-gather.5.cloned.1.call-start = ((), (), s32[]{:S(2)}) async-start(), calls=%async_computation.4 | async-start | bytes 2621440 | tf_op jit(solution)/shard_map/all_gather | solution.py:118
  11.4 165.1 %reduce-scatter.5.cloned.1.call-start = ((), (), s32[]{:S(2)}) async-start(), calls=%async_computation.5 | async-start | bytes 5242880 | tf_op jit(solution)/shard_map/reduce_scatter | solution.py:126
  63.3 5.2 copy-start.1
  85.1 4.5 copy-start.24
  88.2 4.4 copy-start.2
  88.2 4.4 copy-start.39
  100.9 125.8 %all-gather.7.cloned.1.call-start = ((), (), s32[]{:S(2)}) async-start(), calls=%async_computation.6 | async-start | bytes 2621440 | tf_op jit(solution)/shard_map/all_gather | solution.py:134
  180.0 92.8 %all-gather.9.cloned.1.call-start = ((), (), s32[]{:S(2)}) async-start(), calls=%async_computation.8 | async-start | bytes 2621440 | tf_op jit(solution)/shard_map/all_gather | solution.py:148
  180.6 180.2 %reduce-scatter.9.cloned.1.call-start = ((), (), s32[]{:S(2)}) async-start(), calls=%async_computation.9 | async-start | bytes 5242880 | tf_op jit(solution)/shard_map/reduce_scatter | solution.py:158
  226.6 5.3 copy-start.48
  226.6 5.4 copy-start.50
  272.8 6.1 copy-start.51
  285.1 127.0 %all-gather.11.cloned.1.call-start = ((), (), s32[]{:S(2)}) async-start(), calls=%async_computation.10 | async-start | bytes 2621440 | tf_op jit(solution)/shard_map/all_gather | solution.py:167
  365.5 132.7 %reduce-scatter.11.cloned.1.call-start = ((), (), s32[]{:S(2)}) async-start(), calls=%async_computation.11 | async-start | bytes 2621440 | tf_op jit(solution)/shard_map/reduce_scatter | solution.py:176
  420.5 4.5 copy-start.3
  420.5 4.5 copy-start.11
  420.5 4.5 copy-start.29
  455.5 89.4 %reduce-scatter.7.cloned.1.call-start = ((), (), s32[]{:S(2)}) async-start(), calls=%async_computation.7 | async-start | bytes 2621440 | tf_op jit(solution)/shard_map/reduce_scatter | solution.py:141
  460.2 265.9 %all-reduce.8.cloned.1.call-start = ((), (), s32[]{:S(2)}) async-start(), calls=%async_computation.12 | async-start | bytes 25296896 | tf_op jit(solution)/shard_map/psum | solution.py:190
  460.2 5.4 copy-start.49
  460.2 5.4 copy-start.54
  465.6 3.2 copy-start.56
  468.8 3.2 copy-start.30
  478.9 19.3 %copy-start.9 = (bf16[256,1024]{1,0:T(8,128)(2,1)S(1)}, bf16[256,1024]{1,0:T(8,128)(2,1)}, u32[]{:S(2)}) copy-start(bf16[256,1024]{1,0:T(8,128)(2,1)} %param.11) | copy-start | bytes 1572868
  478.9 19.3 %copy-start.42 = (f32[256]{0:T(256)S(1)}, f32[256]{0:T(256)}, u32[]{:S(2)}) copy-start(f32[256]{0:T(256)} %copy-done.41) | copy-start | bytes 3076
  478.9 63.5 %copy-start.46 = (f32[256]{0:T(256)S(1)}, f32[256]{0:T(256)}, u32[]{:S(2)}) copy-start(f32[256]{0:T(256)} %copy-done.45) | copy-start | bytes 3076
  478.9 65.9 %copy-start.6 = (f32[256,1024]{1,0:T(8,128)S(1)}, f32[256,1024]{1,0:T(8,128)}, u32[]{:S(2)}) copy-start(f32[256,1024]{1,0:T(8,128)} %copy-done.4) | copy-start | bytes 3145732
  478.9 65.9 %copy-start.19 = (bf16[256,1024]{1,0:T(8,128)(2,1)S(1)}, bf16[256,1024]{1,0:T(8,128)(2,1)}, u32[]{:S(2)}) copy-start(bf16[256,1024]{1,0:T(8,128)(2,1)} %param.21) | copy-start | bytes 1572868
  479.0 65.9 %copy-start.44 = (f32[256]{0:T(256)S(1)}, f32[256]{0:T(256)}, u32[]{:S(2)}) copy-start(f32[256]{0:T(256)} %copy-done.43) | copy-start | bytes 3076
  726.0 3.4 copy-start.32
  (34 other events, 70.2 us)
Sparse Core Ops, SparseCore 0:
  11.5 48.6 all-gather.4
  101.0 75.4 reduce-scatter.4
  180.1 46.4 all-gather.6
  228.1 44.6 all-gather.8
  285.2 75.4 reduce-scatter.8
  365.6 46.4 all-gather.10
  455.6 42.5 reduce-scatter.10
  500.6 44.2 reduce-scatter.6
  551.0 174.9 all-reduce.7
where the time goes:
time: 756 us; the launch traced here: 746 us
  waiting for transfers between devices  528 us (70%)
  matrix products  76.7 us (10%)
  local copies, waits for them, and re-layouts  62.8 us (8%)
  blocking collectives  42.7 us (6%)
  other arithmetic  20.9 us (3%)
  between operations  14.8 us (2%)
    psum x1, waiting for transfers between devices, local(): lax.psum((grad_query, grad_key, grad_value, grad_out), 'dp')  178 us
    reduce_scatter x1, waiting for transfers between devices, local(): lax.psum_scatter(mat_right(gate_grad, w_gate) + mat_right(up_grad, w_up),...  75.6 us
    reduce_scatter x1, waiting for transfers between devices, local(): lax.psum_scatter(jnp.dot(piece, w_out, preferred_element_type=jnp.float32...  75 us
    all_gather x1, waiting for transfers between devices, local(): normed_all = lax.all_gather(normed_low, 'tensor', axis=0, tiled=True)  47.8 us
    all_gather x1, waiting for transfers between devices, local(): mid_all = lax.all_gather(normed_mid, 'tensor', axis=0, tiled=True)  45.8 us
    all_gather x1, waiting for transfers between devices, local(): lax.all_gather(middle_grad.astype(jnp.bfloat16), 'tensor', axis=0, tiled=...  45.8 us
    psum x1, blocking collectives, local(): gain_totals = lax.psum((attn_gain_part, mlp_gain_part), ('dp', 'tensor'))  42.7 us
    all_gather x1, waiting for transfers between devices, local(): grad_all = lax.all_gather(out_grad, 'tensor', axis=0, tiled=True)  37.6 us
  transfers between devices with their start and end apart: 9, of which 9 were waited for; matrix products, arithmetic and copies ran while one was open for 5% of the time, Pallas kernels for 0%

commit v1 on v0

v1 whole, which is shorter than its diff:
```python
import functools

import jax
import jax.numpy as jnp
from jax import lax
from jax.experimental import pallas as pl
from jax.experimental.pallas import tpu as pltpu
from jax.sharding import PartitionSpec as P

HEAD_DIM = 64
WINDOW = 64
SEQ_LEN = 1024

norm_eps = 1e-05
very_low = -1e30
AXES = ("dp", "tensor")
low = jnp.bfloat16
full = jnp.float32


def mat(left, right):
    return jnp.dot(left, right, preferred_element_type=full)


def mat_left(left, right):
    return lax.dot_general(left, right, (((0,), (0,)), ((), ())), preferred_element_type=full)


def mat_right(left, right):
    return lax.dot_general(left, right, (((1,), (1,)), ((), ())), preferred_element_type=full)


def head_pair(rows):
    lane = lax.broadcasted_iota(jnp.int32, rows.shape, 1)
    zero = jnp.zeros_like(rows)
    return jnp.concatenate(
        [jnp.where(lane < HEAD_DIM, rows, zero), jnp.where(lane < HEAD_DIM, zero, rows)], axis=0
    )


def unstack(stacked):
    half = stacked.shape[0] // 2
    lane = lax.broadcasted_iota(jnp.int32, (half, stacked.shape[1]), 1)
    return jnp.where(lane < HEAD_DIM, stacked[:half], stacked[half:])


def unit_probs(q_stack, keys, first, has_halo):
    scores = mat_right(q_stack, keys) * HEAD_DIM ** (-0.5)
    row = lax.broadcasted_iota(jnp.int32, scores.shape, 0) % WINDOW
    col = lax.broadcasted_iota(jnp.int32, scores.shape, 1)
    mask = (col > row) & (col <= row + WINDOW)
    if first:
        mask = mask & ((col >= WINDOW) | (has_halo > 0))
    scores = jnp.where(mask, scores, very_low)
    expo = jnp.exp(scores - jnp.max(scores, axis=-1, keepdims=True))
    return expo / jnp.sum(expo, axis=-1, keepdims=True)


def attend_kernel(halo_ref, qkv_ref, out_ref):
    seqs, rows, width3 = qkv_ref.shape
    width = width3 // 3
    has_halo = halo_ref[0]
    for seq in range(seqs):
        for lane in range(0, width, 128):
            for top in range(0, rows - WINDOW, WINDOW):
                q = qkv_ref[seq, top + WINDOW : top + 2 * WINDOW, lane : lane + 128]
                k = qkv_ref[seq, top : top + 2 * WINDOW, width + lane : width + lane + 128]
                v = qkv_ref[seq, top : top + 2 * WINDOW, 2 * width + lane : 2 * width + lane + 128]
                probs = unit_probs(head_pair(q), k, top == 0, has_halo).astype(low)
                out_ref[seq, top : top + WINDOW, lane : lane + 128] = unstack(mat(probs, v)).astype(low)


def attend_back_kernel(halo_ref, qkv_ref, grad_ref, out_ref):
    seqs, rows, width3 = qkv_ref.shape
    width = width3 // 3
    has_halo = halo_ref[0]
    factor = HEAD_DIM ** (-0.5)
    for seq in range(seqs):
        for lane in range(0, width, 128):
            out_ref[seq, 0:WINDOW, lane : lane + 128] = jnp.zeros((WINDOW, 128), low)
            k_tail = v_tail = jnp.zeros((WINDOW, 128), full)
            for top in range(0, rows - WINDOW, WINDOW):
                q = head_pair(qkv_ref[seq, top + WINDOW : top + 2 * WINDOW, lane : lane + 128])
                k = qkv_ref[seq, top : top + 2 * WINDOW, width + lane : width + lane + 128]
                v = qkv_ref[seq, top : top + 2 * WINDOW, 2 * width + lane : 2 * width + lane + 128]
                g = head_pair(grad_ref[seq, top : top + WINDOW, lane : lane + 128])
                probs = unit_probs(q, k, top == 0, has_halo)
                prob_grad = mat_right(g, v)
                inner = jnp.sum(probs * prob_grad, axis=-1, keepdims=True)
                score_grad = (probs * (prob_grad - inner)).astype(low)
                q_grad = unstack(mat(score_grad, k)) * factor
                k_grad = mat_left(score_grad, q) * factor
                v_grad = mat_left(probs.astype(low), g)
                out_ref[seq, top + WINDOW : top + 2 * WINDOW, lane : lane + 128] = q_grad.astype(low)
                at = width + lane
                out_ref[seq, top : top + WINDOW, at : at + 128] = (k_tail + k_grad[:WINDOW]).astype(low)
                at = 2 * width + lane
                out_ref[seq, top : top + WINDOW, at : at + 128] = (v_tail + v_grad[:WINDOW]).astype(low)
                k_tail, v_tail = k_grad[WINDOW:], v_grad[WINDOW:]
            at = width + lane
            out_ref[seq, rows - WINDOW : rows, at : at + 128] = k_tail.astype(low)
            at = 2 * width + lane
            out_ref[seq, rows - WINDOW : rows, at : at + 128] = v_tail.astype(low)


def attend(has_halo, qkv):
    seqs, rows, width3 = qkv.shape
    work = seqs * rows * width3
    return pl.pallas_call(
        attend_kernel,
        out_shape=jax.ShapeDtypeStruct((seqs, rows - WINDOW, width3 // 3), low),
        in_specs=[pl.BlockSpec(memory_space=pltpu.SMEM), pl.BlockSpec(memory_space=pltpu.VMEM)],
        out_specs=pl.BlockSpec(memory_space=pltpu.VMEM),
        compiler_params=pltpu.CompilerParams(vmem_limit_bytes=16 << 20),
        cost_estimate=pl.CostEstimate(flops=work * 512, bytes_accessed=work * 3, transcendentals=work),
    )(has_halo, qkv)


def attend_back(has_halo, qkv, grad):
    work = qkv.size
    return pl.pallas_call(
        attend_back_kernel,
        out_shape=jax.ShapeDtypeStruct(qkv.shape, low),
        in_specs=[pl.BlockSpec(memory_space=pltpu.SMEM)] + [pl.BlockSpec(memory_space=pltpu.VMEM)] * 2,
        out_specs=pl.BlockSpec(memory_space=pltpu.VMEM),
        compiler_params=pltpu.CompilerParams(vmem_limit_bytes=16 << 20),
        cost_estimate=pl.CostEstimate(flops=work * 1024, bytes_accessed=work * 5, transcendentals=work),
    )(has_halo, qkv, grad)


def rms_scale(values):
    return lax.rsqrt(jnp.mean(values * values, axis=-1, keepdims=True) + norm_eps)


def rms_norm(values, gain):
    return values * rms_scale(values) * gain


def rms_pull(values, gain, grad):
    scale = rms_scale(values)
    unit = values * scale
    scaled = grad * gain
    inner = jnp.mean(scaled * unit, axis=-1, keepdims=True)
    return scale * (scaled - unit * inner), jnp.sum(grad * unit, axis=0)


def build(n_dp, n_t):
    bits = [1 << k for k in range(1, n_dp.bit_length() - 1)]
    rounds = len(bits)
    quarters = 1 << rounds

    def perm(target):
        pairs = []
        for d in range(n_dp):
            for t in range(n_t):
                to = target(d, t)
                if to is not None:
                    pairs.append((d * n_t + t, to[0] * n_t + to[1]))
        return pairs

    def order(which):
        return bits if which == 0 else bits[::-1]

    send_core = functools.partial(lax.ppermute, axis_name=AXES, perm=perm(lambda d, t: (d ^ 1, t)))
    send_pair = functools.partial(lax.ppermute, axis_name=AXES, perm=perm(lambda d, t: (d, t ^ 1)))
    send_far = functools.partial(lax.ppermute, axis_name=AXES, perm=perm(lambda d, t: (d, t ^ 2)))

    def local(
        tokens, gain_attn, w_query, w_key, w_value, w_out, gain_mlp, w_gate, w_up, w_down, out_grad
    ):
        own_rows, depth = tokens.shape
        hidden_cols = w_gate.shape[1]
        head_cols = w_query.shape[1]
        d, t = lax.axis_index("dp"), lax.axis_index("tensor")
        core, part, side = d & 1, t & 1, t >> 1
        resident = core == side

        def bit_of(bit):
            return (d // bit) & 1

        def ordered(index, mine, other, axis=0):
            first = jnp.where(index == 0, mine, other)
            second = jnp.where(index == 0, other, mine)
            return jnp.concatenate([first, second], axis=axis)

        def pick(array, index):
            return lax.dynamic_index_in_dim(array, index, 0, keepdims=False)

        def double(piece, sequence_of, index_of):
            for i in range(rounds):
                way = perm(lambda d_, t_: (d_ ^ sequence_of(d_ & 1, t_ >> 1)[i], t_))
                piece = ordered(index_of(i), piece[None], lax.ppermute(piece, AXES, way)[None])
                piece = piece.reshape((-1,) + piece.shape[2:]) if i else piece
            return piece

        def select_bit(i, lists):
            return jnp.where(core == 0, bit_of(lists[0][i]), bit_of(lists[1][i]))

        def untranspose(stack):
            rest = stack.shape[1:]
            dims = tuple(range(rounds - 1, -1, -1)) + tuple(range(rounds, rounds + len(rest)))
            return stack.reshape((2,) * rounds + rest).transpose(dims).reshape(stack.shape)

        def fetch(pieces):
            index = 0
            for bit in bits[::-1]:
                index = index * 2 + bit_of(bit)
            piece = pick(pieces, index * 2 + core)
            piece = lax.ppermute(piece, AXES, perm(lambda d_, t_: (d_, t_ ^ 2)))
            lists = (bits, bits[::-1])
            stack = double(
                piece, lambda c_, h_: lists[c_], lambda i: select_bit(i, lists)
            )
            other = lax.ppermute(
                stack, AXES, perm(lambda d_, t_: (d_ ^ 1, t_) if (d_ & 1) == (t_ >> 1) else None)
            )
            zero = jnp.where(core == 0, stack, other)
            one = untranspose(jnp.where(core == 0, other, stack))
            both = jnp.stack([zero, one], axis=1)
            return both.reshape(pieces.shape)

        def rows_in(array):
            return array.reshape((2 * quarters, array.shape[0] // (2 * quarters)) + array.shape[1:])

        def columns_in(array):
            return array.reshape(array.shape[0], 2 * quarters, -1).transpose(1, 0, 2)

        def columns_out(pieces):
            return pieces.transpose(1, 0, 2).reshape(pieces.shape[1], -1)

        def gather_group(rows):
            pair = ordered(part, rows, send_pair(rows))
            return ordered(core, pair, send_core(pair))

        def scatter_group(make):
            theirs = make(1 - core).astype(low)
            arrived = send_core(theirs)
            mine = make(core) + arrived.astype(full)
            halves = mine.reshape(2, -1, mine.shape[-1])
            arrived = send_pair(pick(halves, 1 - part).astype(low))
            return pick(halves, part) + arrived.astype(full)

        def reduce_slice(pieces):
            lists = (bits, bits[::-1])
            stack = pieces
            for i in range(rounds):
                bit = select_bit(i, lists)
                halves = stack.reshape((2, stack.shape[0] // 2) + stack.shape[1:])
                way = perm(lambda d_, t_: (d_ ^ lists[d_ & 1][i], t_))
                arrived = lax.ppermute(pick(halves, 1 - bit).astype(low), AXES, way)
                stack = pick(halves, bit).astype(full) + arrived.astype(full)
            piece = stack[0]
            arrived = lax.ppermute(
                piece.astype(low),
                AXES,
                perm(lambda d_, t_: (d_, t_ ^ 2) if (d_ & 1) != (t_ >> 1) else None),
            )
            total = (piece + arrived.astype(full)).astype(low)
            halves = total.reshape((2, total.shape[0] // 2) + total.shape[1:])
            arrived = lax.ppermute(
                pick(halves, 1 - core),
                AXES,
                perm(lambda d_, t_: (d_ ^ 1, t_) if (d_ & 1) == (t_ >> 1) else None),
            )
            half = jnp.where(resident, pick(halves, core), arrived)
            def back(c_, h_):
                return lists[h_][::-1] if c_ == 0 else lists[h_]

            def back_bit(i):
                up = jnp.where(side == 0, bit_of(lists[0][i]), bit_of(lists[1][i]))
                down = jnp.where(
                    side == 0, bit_of(lists[0][rounds - 1 - i]), bit_of(lists[1][rounds - 1 - i])
                )
                return jnp.where(core == 0, down, up)

            stack = double(half, back, back_bit)
            other = send_core(stack)
            zero = jnp.where(core == 0, stack, other)
            one = untranspose(jnp.where(core == 0, other, stack))
            both = jnp.stack([zero, one], axis=1)
            return both

        tail = tokens[own_rows - WINDOW :]
        halo = lax.ppermute(
            tail, AXES, perm(lambda d_, t_: (d_, 2) if t_ == 1 else None)
        ) + lax.ppermute(tail, AXES, perm(lambda d_, t_: (d_, 3) if t_ == 1 else None))
        mine = jnp.concatenate([halo, ordered(part, tokens, send_pair(tokens))], axis=0)
        seqs = ordered(core, mine[None], send_core(mine)[None])

        own_qkv = jnp.concatenate([w_query, w_key, w_value], axis=1)
        far_qkv = fetch(rows_in(own_qkv)).reshape(own_qkv.shape)
        qkv_weight = jnp.where(resident, own_qkv, far_qkv)

        own_deep = columns_in(jnp.concatenate([w_out, w_down], axis=0))
        deep = columns_out(jnp.where(resident, own_deep, fetch(own_deep)))
        out_weight, down_weight = deep[:head_cols], deep[head_cols:]

        own_wide = jnp.stack([rows_in(w_gate), rows_in(w_up)], axis=1)
        wide = jnp.where(resident, own_wide, fetch(own_wide))
        gate_weight = wide[:, 0].reshape(depth, hidden_cols)
        up_weight = wide[:, 1].reshape(depth, hidden_cols)

        attn_gain = gain_attn.astype(full)
        mlp_gain = gain_mlp.astype(full)
        has_halo = jnp.reshape(side, (1,)).astype(jnp.int32)

        normed = rms_norm(seqs.astype(full), attn_gain).astype(low)
        ext = normed.shape[1]
        normed_flat = normed.reshape(2 * ext, depth)
        qkv = mat(normed_flat, qkv_weight).astype(low).reshape(2, ext, 3 * head_cols)
        attended = attend(has_halo, qkv)
        branch = scatter_group(lambda which: mat(pick(attended, which), out_weight))
        token_float = tokens.astype(full)
        middle = token_float + branch

        normed_mid = rms_norm(middle, mlp_gain).astype(low)
        mid_all = gather_group(normed_mid)
        grad_all = gather_group(out_grad)
        gate_pre = mat(mid_all, gate_weight)
        up_pre = mat(mid_all, up_weight)
        gate_sig = jax.nn.sigmoid(gate_pre)
        silu_val = gate_pre * gate_sig
        hidden = (silu_val * up_pre).astype(low)
        hidden_grad = mat_right(grad_all, down_weight)
        up_grad = (hidden_grad * silu_val).astype(low)
        gate_grad = (hidden_grad * up_pre * gate_sig * (1.0 + gate_pre * (1.0 - gate_sig))).astype(low)

        def core_rows(array, which):
            return pick(array.reshape((2, -1) + array.shape[1:]), which)

        mid_grad = scatter_group(
            lambda which: mat_right(core_rows(gate_grad, which), gate_weight)
            + mat_right(core_rows(up_grad, which), up_weight)
        )
        mid_pull, mlp_gain_part = rms_pull(middle, mlp_gain, mid_grad)
        middle_grad = out_grad.astype(full) + mid_pull

        mlp_out = scatter_group(lambda which: mat(core_rows(hidden, which), down_weight))
        output = (middle + mlp_out).astype(low)

        down_part = mat_left(hidden, grad_all).astype(low)
        down_part = down_part.reshape(hidden_cols, quarters, 2, -1).transpose(1, 2, 0, 3)
        grad_down = reduce_slice(down_part)
        grad_down = grad_down.reshape((2 * quarters,) + grad_down.shape[3:])
        grad_down = columns_out(grad_down).astype(full)

        wide_part = jnp.stack(
            [
                mat_left(mid_all, gate_grad).astype(low).reshape(quarters, 2, -1, hidden_cols),
                mat_left(mid_all, up_grad).astype(low).reshape(quarters, 2, -1, hidden_cols),
            ],
            axis=2,
        )
        wide_sum = reduce_slice(wide_part)
        wide_sum = wide_sum.reshape((2 * quarters, 2) + wide_sum.shape[4:])
        grad_gate = wide_sum[:, 0].reshape(depth, hidden_cols).astype(full)
        grad_up = wide_sum[:, 1].reshape(depth, hidden_cols).astype(full)

        branch_all = gather_group(middle_grad.astype(low))
        attended_grad = mat_right(branch_all, out_weight).astype(low).reshape(attended.shape)
        qkv_grad = attend_back(has_halo, qkv, attended_grad)
        qkv_grad_flat = qkv_grad.reshape(2 * ext, 3 * head_cols)
        attn_part = jnp.concatenate(
            [
                mat_left(normed_flat, qkv_grad_flat),
                mat_left(branch_all, attended.reshape(-1, head_cols)),
            ],
            axis=1,
        ).astype(low)
        attn_sum = reduce_slice(attn_part.reshape(quarters, 2, -1, 4 * head_cols))
        attn_sum = attn_sum.reshape(depth, 4 * head_cols).astype(full)
        grad_query = attn_sum[:, :head_cols]
        grad_key = attn_sum[:, head_cols : 2 * head_cols]
        grad_value = attn_sum[:, 2 * head_cols : 3 * head_cols]
        grad_out = attn_sum[:, 3 * head_cols :].T

        arrived = send_core(mat_right(pick(qkv_grad, 1 - core), qkv_weight).astype(low))
        mine = mat_right(pick(qkv_grad, core), qkv_weight) + arrived.astype(full)
        halo_part = mine[:WINDOW]
        halves = mine[WINDOW:].reshape(2, own_rows, depth)
        arrived = send_pair(
            jnp.concatenate([halo_part, pick(halves, 1 - part)], axis=0).astype(low)
        ).astype(full)
        halo_grad = lax.ppermute(
            (halo_part + arrived[:WINDOW]).astype(low),
            AXES,
            perm(lambda d_, t_: (d_, 1) if t_ == 2 else None),
        ).astype(full)
        normed_grad = pick(halves, part) + arrived[WINDOW:]
        normed_grad = jnp.concatenate(
            [normed_grad[: own_rows - WINDOW], normed_grad[own_rows - WINDOW :] + halo_grad], axis=0
        )
        token_pull, attn_gain_part = rms_pull(token_float, attn_gain, normed_grad)
        input_grad = middle_grad + token_pull
        gain_totals = lax.psum(jnp.stack([attn_gain_part, mlp_gain_part]), AXES)
        return (
            output,
            input_grad,
            gain_totals[0],
            grad_query,
            grad_key,
            grad_value,
            grad_out,
            gain_totals[1],
            grad_gate,
            grad_up,
            grad_down,
        )

    return local


def solution(mesh):
    both = P(("dp", "tensor"), None)
    columns, rows = P(None, "tensor"), P("tensor", None)
    return jax.shard_map(
        build(mesh.shape["dp"], mesh.shape["tensor"]),
        mesh=mesh,
        in_specs=(both, P(), columns, columns, columns, rows, P(), columns, columns, rows, both),
        out_specs=(both, both, P(), columns, columns, columns, rows, P(), columns, columns, rows),
        check_vma=False,
    )
```

time: 756 us -> 444 us (0.59)
  waiting for transfers between devices: 528 us -> 144 us
  starting transfers between devices: 0.54 us -> 61.7 us
  matrix products: 76.7 us -> 41.2 us
  Pallas kernels: 0 us -> 24.1 us
  other arithmetic: 20.9 us -> 42.4 us
  local copies, waits for them, and re-layouts: 62.8 us -> 79.5 us
  between operations: 14.8 us -> 2.81 us
    psum x1 -> x0, waiting for transfers between devices: 178 us -> none  [local(): lax.psum((grad_query, grad_key, grad_value, grad_out), 'dp')]
    all_gather x4 -> x0, waiting for transfers between devices: 177 us -> none  [the longest x1 47.8 us: local(): normed_all = lax.all_gather(normed_low, 'tensor', axis=0, tiled=True)]
    reduce_scatter x4 -> x0, waiting for transfers between devices: 172 us -> none  [the longest x1 75.6 us: local(): lax.psum_scatter(mat_right(gate_grad, w_gate) + mat_right(up_grad, w_up),...]
    ppermute x0 -> x52, waiting for transfers between devices: none -> 144 us  [the longest x12 32.8 us: double(): lax.ppermute(piece, AXES, way)[None]]
    ppermute x0 -> x52, starting transfers between devices: none -> 61.7 us  [the longest x12 17.1 us: double(): lax.ppermute(piece, AXES, way)[None]]
    dot_general x13 -> x7, matrix products: 38.1 us -> 10.8 us  [mat(): return jnp.dot(left, right, preferred_element_type=full)]
    pallas_call x0 -> x2, Pallas kernels: none -> 24.1 us  [the longest x1 13.8 us: attend_back(): pl.pallas_call(attend_back_kernel, out_shape=jax.ShapeDtypeStruct(qkv.sha...]
    select_n x0 -> x28, other arithmetic: none -> 14.2 us  [the longest x20 13.1 us: ordered(): first = jnp.where(index == 0, mine, other)]
  transfers between devices with their start and end apart: 9 -> 52, of which waited for: 9 -> 21; matrix products, arithmetic and copies ran while one was open for 5% -> 24% of each run, Pallas kernels for 0% -> 5%
where the time goes in v1:
time: 444 us; the launch traced here: 439 us
  waiting for transfers between devices  144 us (32%)
  local copies, waits for them, and re-layouts  79.5 us (18%)
  starting transfers between devices  61.7 us (14%)
  blocking collectives  43.3 us (10%)
  other arithmetic  42.4 us (10%)
  matrix products  41.2 us (9%)
  Pallas kernels  24.1 us (5%)
    psum x1, blocking collectives, local(): gain_totals = lax.psum(jnp.stack([attn_gain_part, mlp_gain_part]), AXES)  43.3 us
    ppermute x12, waiting for transfers between devices, double(): lax.ppermute(piece, AXES, way)[None]  32.8 us
    ppermute x3, waiting for transfers between devices, reduce_slice(): lax.ppermute(piece.astype(low), AXES, perm(lambda d_, t_: (d_, t_ ^ 2) if...  31.6 us
    ppermute x3, waiting for transfers between devices, gather_group(): pair = ordered(part, rows, send_pair(rows))  22.3 us
    ppermute x6, waiting for transfers between devices, reduce_slice(): arrived = lax.ppermute(pick(halves, 1 - bit).astype(low), AXES, way)  18.9 us
    dot_general x5, matrix products, mat_left(): lax.dot_general(left, right, (((0,), (0,)), ((), ())), preferred_element_...  18.1 us
    ppermute x12, starting transfers between devices, double(): lax.ppermute(piece, AXES, way)[None]  17.1 us
    unnamed x106, local copies, waits for them, and re-layouts  15.2 us
  transfers between devices with their start and end apart: 52, of which 21 were waited for; matrix products, arithmetic and copies ran while one was open for 24% of the time, Pallas kernels for 5%

profile of v1, /device:TPU:0, one launch (start us, length us, event | category | flops | bytes accessed | tf_op | source)
XLA Modules:
  0.0 439.0 jit_solution(2091540267836489790)
XLA Ops:
  2.3 4.1 collective-permute-start.4
  9.3 12.3 %collective-permute-done.4 = bf16[128,768]{1,0:T(8,128)(2,1)S(1)} collective-permute-done((bf16[128,768]{1,0:T(8,128)(2,1)S(1)}, bf16[128,768]{1,0:T(8,128)(2,1)S(1)}, u32[]{:S(2)}, u32[]{:S(2)}) %collective-permute-start.4) | collective-permute-done | bytes 196640 | tf_op jit(solution)/shard_map/ppermute | solution.py:209
  25.4 4.9 %collective-permute-start.2 = (bf16[256,1024]{1,0:T(8,128)(2,1)S(1)}, bf16[256,1024]{1,0:T(8,128)(2,1)S(1)}, u32[]{:S(2)}, u32[]{:S(2)}) collective-permute-start(bf16[256,1024]{1,0:T(8,128)(2,1)S(1)} %copy-done.7), channel_id=1, source_target_pairs={{0,1},{1,0},{2,3},{3,2},{4,5},{5,4},{6,7},{7,6},{8,9},{9,8},{10,11... | collective-permute-start | bytes 1572872 | tf_op jit(solution)/shard_map/ppermute | solution.py:287
  34.9 5.5 %collective-permute-done.9 = bf16[944,128]{1,0:T(8,128)(2,1)S(1)} collective-permute-done((bf16[944,128]{1,0:T(8,128)(2,1)S(1)}, bf16[944,128]{1,0:T(8,128)(2,1)S(1)}, u32[]{:S(2)}, u32[]{:S(2)}) %collective-permute-start.9) | collective-permute-done | bytes 241696 | tf_op jit(solution)/shard_map/ppermute | solution.py:192
  55.1 4.4 collective-permute-start.11
  66.9 10.3 %shard_map.194 = bf16[2,512,256]{2,1,0:T(8,128)(2,1)S(1)} custom-call(s32[1]{0:T(128)} %bitcast.halo_ref, bf16[2,576,768]{2,1,0:T(8,128)(2,1)S(1)} %bitcast.371), custom_call_target="tpu_custom_call" | custom-call | flops 452984832 | bytes 2654208 | tf_op jit(solution)/shard_map/pallas_call | solution.py:109
  87.0 5.6 %collective-permute-done.17 = bf16[2,128,688]{1,2,0:T(8,128)(2,1)} collective-permute-done((bf16[2,128,688]{1,2,0:T(8,128)(2,1)}, bf16[2,128,688]{1,2,0:T(8,128)(2,1)}, u32[]{:S(2)}, u32[]{:S(2)}) %collective-permute-start.17) | collective-permute-done | bytes 352288 | tf_op jit(solution)/shard_map/ppermute | solution.py:192
  96.0 5.2 %collective-permute-done.22 = bf16[256,1024]{1,0:T(8,128)(2,1)} collective-permute-done((bf16[256,1024]{1,0:T(8,128)(2,1)S(1)}, bf16[256,1024]{1,0:T(8,128)(2,1)}, u32[]{:S(2)}, u32[]{:S(2)}) %collective-permute-start.22) | collective-permute-done | bytes 524320 | tf_op jit(solution)/shard_map/ppermute | solution.py:232
  111.0 7.3 %collective-permute-done.13 = bf16[256,1024]{1,0:T(8,128)(2,1)S(1)} collective-permute-done((bf16[256,1024]{1,0:T(8,128)(2,1)S(1)}, bf16[256,1024]{1,0:T(8,128)(2,1)S(1)}, u32[]{:S(2)}, u32[]{:S(2)}) %collective-permute-start.13) | collective-permute-done | bytes 524320 | tf_op jit(solution)/shard_map/ppermute | solution.py:240
  122.2 10.4 %collective-permute-done.14 = bf16[256,1024]{1,0:T(8,128)(2,1)} collective-permute-done((bf16[256,1024]{1,0:T(8,128)(2,1)}, bf16[256,1024]{1,0:T(8,128)(2,1)}, u32[]{:S(2)}, u32[]{:S(2)}) %collective-permute-start.14) | collective-permute-done | bytes 524320 | tf_op jit(solution)/shard_map/ppermute | solution.py:232
  143.7 5.3 %multiply_convert_fusion = (bf16[1024,688]{0,1:T(8,128)(2,1)}, bf16[1024,688]{0,1:T(8,128)(2,1)S(1)}, bf16[1024,688]{0,1:T(8,128)(2,1)}) fusion(f32[1024,688]{0,1:T(8,128)S(1)} %fusion.23, f32[1024,688]{0,1:T(8,128)S(1)} %fusion.17, bf16[86,8,8,128]{3,2,1,0:T(8,128)(2,1)S(1)} %bitcast.433, bf16[512,1024]{1,0:T(8,128)(2,1)S(1)} %get-tuple-element.85, ...), kind=kOutput, calls=%fused_computation.13 | convolution fusion | flops 1457602560 | bytes 13369344 | tf_op jit(solution)/shard_map/dot_general | solution.py:30
  153.0 4.6 %reshape.645 = bf16[2,512,688]{1,0,2:T(2,128)(2,1)} reshape(bf16[1024,688]{0,1:T(8,128)(2,1)} %copy-done.37) | data formatting | bytes 2818048 | tf_op jit(solution)/shard_map/reshape | solution.py:329
  157.6 4.7 %convolution_convert_fusion.1 = bf16[1024,688]{0,1:T(8,128)(2,1)} fusion(bf16[1024,688]{0,1:T(8,128)(2,1)} %get-tuple-element.63, bf16[512,1024]{1,0:T(8,128)(2,1)} %copy-done.44, bf16[512,1024]{1,0:T(8,128)(2,1)} %copy-done.43), kind=kOutput, calls=%fused_computation.38 | convolution fusion | flops 1447739392 | bytes 4915200 | tf_op jit(solution)/shard_map/dot_general | solution.py:26
  162.3 4.6 %reshape.646 = bf16[2,512,688]{1,0,2:T(2,128)(2,1)} reshape(bf16[1024,688]{0,1:T(8,128)(2,1)} %get-tuple-element.63) | data formatting | bytes 2818048 | tf_op jit(solution)/shard_map/reshape | solution.py:329
  166.9 4.7 %convolution_convert_fusion.3 = bf16[688,1024]{1,0:T(8,128)(2,1)} fusion(bf16[1024,688]{0,1:T(8,128)(2,1)} %get-tuple-element.65, bf16[512,1024]{1,0:T(8,128)(2,1)} %copy-done.42, bf16[512,1024]{1,0:T(8,128)(2,1)} %copy-done.41), kind=kOutput, calls=%fused_computation.40 | convolution fusion | flops 1447739392 | bytes 4915200 | tf_op jit(solution)/shard_map/dot_general | solution.py:26
  171.6 4.6 %reshape.643 = bf16[2,512,688]{1,0,2:T(2,128)(2,1)} reshape(bf16[1024,688]{0,1:T(8,128)(2,1)} %get-tuple-element.65) | data formatting | bytes 2818048 | tf_op jit(solution)/shard_map/reshape | solution.py:329
  176.2 5.0 %reshape.656 = bf16[688,4,2,128]{3,2,1,0:T(2,128)(2,1)} reshape(bf16[688,1024]{1,0:T(8,128)(2,1)} %convolution_convert_fusion.3) | data formatting | bytes 2818048 | tf_op jit(solution)/shard_map/reshape | solution.py:342
  186.9 4.6 %stack.67 = bf16[2,2,2,1,128,688]{4,2,1,0,5,3:T(2,128)(2,1)} reshape(bf16[1024,688]{0,1:T(8,128)(2,1)} %convolution_convert_fusion.2) | data formatting | bytes 2818048 | tf_op jit(solution)/shard_map/stack | solution.py:347
  191.5 4.6 %stack.68 = bf16[2,2,2,1,128,688]{4,2,1,0,5,3:T(2,128)(2,1)} reshape(bf16[1024,688]{0,1:T(8,128)(2,1)} %convolution_convert_fusion.1) | data formatting | bytes 2818048 | tf_op jit(solution)/shard_map/stack | solution.py:347
  202.6 6.0 %constant_dynamic-slice_fusion.5 = (bf16[1,512,688]{1,0,2:T(2,128)(2,1)S(1)}, bf16[1,512,688]{1,0,2:T(2,128)(2,1)S(1)}, bf16[1,512,688]{1,0,2:T(2,128)(2,1)S(1)}, bf16[1,512,688]{1,0,2:T(2,128)(2,1)S(1)}) fusion(bf16[2,512,688]{1,0,2:T(2,128)(2,1)S(1)} %copy-done.4, s32[]{:T(128)S(6)} %select_n.733, s32[]{:T(128)S(6)} %select_n.749, ...), kind=kLoop, calls=%fused_computation.242 | loop fusion | bytes 5636104 | tf_op jit(solution)/shard_map/jit(dynamic_index_in_dim)/dynamic_slice | solution.py:187
  218.0 7.9 %collective-permute-done.46 = bf16[1,2,688,128]{3,2,1,0:T(8,128)(2,1)S(1)} collective-permute-done((bf16[1,2,688,128]{3,2,1,0:T(8,128)(2,1)S(1)}, bf16[1,2,688,128]{3,2,1,0:T(8,128)(2,1)S(1)}, u32[]{:S(2)}, u32[]{:S(2)}) %collective-permute-start.46) | collective-permute-done | bytes 352288 | tf_op jit(solution)/shard_map/ppermute | solution.py:250
  228.9 11.0 %collective-permute-done.47 = bf16[2,688,128]{2,1,0:T(8,128)(2,1)S(1)} collective-permute-done((bf16[2,688,128]{2,1,0:T(8,128)(2,1)S(1)}, bf16[2,688,128]{2,1,0:T(8,128)(2,1)S(1)}, u32[]{:S(2)}, u32[]{:S(2)}) %collective-permute-start.47) | collective-permute-done | bytes 352288 | tf_op jit(solution)/shard_map/ppermute | solution.py:253
  241.8 4.5 %collective-permute-done.21 = bf16[256,1024]{1,0:T(8,128)(2,1)S(1)} collective-permute-done((bf16[256,1024]{1,0:T(8,128)(2,1)S(1)}, bf16[256,1024]{1,0:T(8,128)(2,1)S(1)}, u32[]{:S(2)}, u32[]{:S(2)}) %collective-permute-start.21) | collective-permute-done | bytes 524320 | tf_op jit(solution)/shard_map/ppermute | solution.py:240
  254.4 6.6 %collective-permute-done.26 = bf16[256,1024]{1,0:T(8,128)(2,1)S(1)} collective-permute-done((bf16[256,1024]{1,0:T(8,128)(2,1)S(1)}, bf16[256,1024]{1,0:T(8,128)(2,1)S(1)}, u32[]{:S(2)}, u32[]{:S(2)}) %collective-permute-start.26) | collective-permute-done | bytes 524320 | tf_op jit(solution)/shard_map/ppermute | solution.py:232
  267.3 19.1 %collective-permute-done.40 = bf16[2,2,128,688]{2,3,1,0:T(8,128)(2,1)S(1)} collective-permute-done((bf16[2,2,128,688]{2,3,1,0:T(8,128)(2,1)S(1)}, bf16[2,2,128,688]{2,3,1,0:T(8,128)(2,1)S(1)}, u32[]{:S(2)}, u32[]{:S(2)}) %collective-permute-start.40) | collective-permute-done | bytes 704544 | tf_op jit(solution)/shard_map/ppermute | solution.py:253
  291.2 13.8 %shard_map.195 = bf16[2,576,768]{2,1,0:T(8,128)(2,1)S(1)} custom-call(s32[1]{0:T(128)} %bitcast.halo_ref, bf16[2,576,768]{2,1,0:T(8,128)(2,1)S(1)} %bitcast.372, bf16[2,512,256]{2,1,0:T(8,128)(2,1)S(1)} %bitcast.374), custom_call_target="tpu_custom_call" | custom-call | flops 905969664 | bytes 4423680 | tf_op jit(solution)/shard_map/pallas_call | solution.py:121
  318.7 4.4 collective-permute-done.42
  327.9 7.4 %collective-permute-done.31 = bf16[2,2,128,1024]{3,2,1,0:T(8,128)(2,1)S(1)} collective-permute-done((bf16[2,2,128,1024]{3,2,1,0:T(8,128)(2,1)S(1)}, bf16[2,2,128,1024]{3,2,1,0:T(8,128)(2,1)S(1)}, u32[]{:S(2)}, u32[]{:S(2)}) %collective-permute-start.31) | collective-permute-done | bytes 1048608 | tf_op jit(solution)/shard_map/ppermute | solution.py:250
  336.9 7.3 %collective-permute-done.43 = bf16[2,1,2,128,688]{3,4,2,0,1:T(8,128)(2,1)S(1)} collective-permute-done((bf16[2,1,2,128,688]{3,4,2,0,1:T(8,128)(2,1)S(1)}, bf16[2,1,2,128,688]{3,4,2,0,1:T(8,128)(2,1)S(1)}, u32[]{:S(2)}, u32[]{:S(2)}) %collective-permute-start.43) | collective-permute-done | bytes 704544 | tf_op jit(solution)/shard_map/ppermute | solution.py:192
  347.7 14.3 %collective-permute-done.29 = bf16[320,1024]{1,0:T(8,128)(2,1)S(1)} collective-permute-done((bf16[320,1024]{1,0:T(8,128)(2,1)S(1)}, bf16[320,1024]{1,0:T(8,128)(2,1)S(1)}, u32[]{:S(2)}, u32[]{:S(2)}) %collective-permute-start.29) | collective-permute-done | bytes 655392 | tf_op jit(solution)/shard_map/ppermute | solution.py:381
  368.2 43.3 %psum.7 = f32[2,1024]{1,0:T(2,128)S(1)} all-reduce(f32[2,1024]{1,0:T(2,128)S(1)} %pad_maximum_fusion.31), channel_id=1, replica_groups=mesh['dp'=8,'tensor'=4] {'dp','tensor'}, use_global_device_ids=true, to_apply=%region_7.8 | all-reduce | flops 2048 | bytes 16384 | tf_op jit(solution)/shard_map/psum | solution.py:395
  422.7 5.0 %collective-permute-done.36 = bf16[2,1,128,1024]{3,2,0,1:T(8,128)(2,1)S(1)} collective-permute-done((bf16[2,1,128,1024]{3,2,0,1:T(8,128)(2,1)S(1)}, bf16[2,1,128,1024]{3,2,0,1:T(8,128)(2,1)S(1)}, u32[]{:S(2)}, u32[]{:S(2)}) %collective-permute-start.36) | collective-permute-done | bytes 524320 | tf_op jit(solution)/shard_map/ppermute | solution.py:192
  (344 shorter events, 172.6 us)
Async XLA Ops:
  2.3 19.2 %collective-permute-start.4 = (bf16[128,768]{1,0:T(8,128)(2,1)S(1)}, bf16[128,768]{1,0:T(8,128)(2,1)S(1)}, u32[]{:S(2)}, u32[]{:S(2)}) collective-permute-start(bf16[128,768]{1,0:T(8,128)(2,1)S(1)} %dynamic-slice_bitcast_fusion.2), channel_id=1, source_target_pairs={{0,2},{1,3},{2,0},{3,1},{4,6},{5,7},{6,4},{7,5},{8,10},{9,11},{10,... | collective-permute-start | bytes 589832 | tf_op jit(solution)/shard_map/ppermute | solution.py:209
  9.0 22.7 %collective-permute-start.8 = (bf16[944,128]{1,0:T(8,128)(2,1)S(1)}, bf16[944,128]{1,0:T(8,128)(2,1)S(1)}, u32[]{:S(2)}, u32[]{:S(2)}) collective-permute-start(bf16[944,128]{1,0:T(8,128)(2,1)S(1)} %bitcast.441), channel_id=1, source_target_pairs={{0,2},{1,3},{2,0},{3,1},{4,6},{5,7},{6,4},{7,5},{8,10},{9,11},{10,... | collective-permute-start | bytes 725000 | tf_op jit(solution)/shard_map/ppermute | solution.py:209
  25.4 18.3 %collective-permute-start.2 = (bf16[256,1024]{1,0:T(8,128)(2,1)S(1)}, bf16[256,1024]{1,0:T(8,128)(2,1)S(1)}, u32[]{:S(2)}, u32[]{:S(2)}) collective-permute-start(bf16[256,1024]{1,0:T(8,128)(2,1)S(1)} %copy-done.7), channel_id=1, source_target_pairs={{0,1},{1,0},{2,3},{3,2},{4,5},{5,4},{6,7},{7,6},{8,9},{9,8},{10,11... | collective-permute-start | bytes 1572872 | tf_op jit(solution)/shard_map/ppermute | solution.py:287
  44.9 16.3 %collective-permute-start.3 = (bf16[576,1024]{1,0:T(8,128)(2,1)}, bf16[576,1024]{1,0:T(8,128)(2,1)}, u32[]{:S(2)}, u32[]{:S(2)}) collective-permute-start(bf16[576,1024]{1,0:T(8,128)(2,1)} %pad_maximum_fusion.15), channel_id=1, source_target_pairs={{0,4},{1,5},{2,6},{3,7},{4,0},{5,1},{6,2},{7,3},{8,12},{9,13},{10,... | collective-permute-start | bytes 3538952 | tf_op jit(solution)/shard_map/ppermute | solution.py:288
  45.1 14.3 %collective-permute-start.7 = (bf16[4,128,768]{2,1,0:T(8,128)(2,1)S(1)}, bf16[4,128,768]{2,1,0:T(8,128)(2,1)}, u32[]{:S(2)}, u32[]{:S(2)}) collective-permute-start(bf16[4,128,768]{2,1,0:T(8,128)(2,1)S(1)} %bitcast.417), channel_id=1, source_target_pairs={{0,4},{1,5},{6,2},{7,3},{8,12},{9,13},{14,10},{15,11},{16,20},{17,... | collective-permute-start | bytes 2359304 | tf_op jit(solution)/shard_map/ppermute | solution.py:214
  52.3 32.7 %collective-permute-start.16 = (bf16[2,128,688]{1,2,0:T(8,128)(2,1)}, bf16[2,128,688]{1,2,0:T(8,128)(2,1)}, u32[]{:S(2)}, u32[]{:S(2)}) collective-permute-start(bf16[2,128,688]{1,2,0:T(8,128)(2,1)} %bitcast.369), channel_id=1, source_target_pairs={{0,2},{1,3},{2,0},{3,1},{4,6},{5,7},{6,4},{7,5},{8,10},{9,11},{10,... | collective-permute-start | bytes 1056776 | tf_op jit(solution)/shard_map/ppermute | solution.py:209
  55.1 22.2 %collective-permute-start.11 = (bf16[4,944,128]{2,1,0:T(8,128)(2,1)S(1)}, bf16[4,944,128]{2,1,0:T(8,128)(2,1)S(1)}, u32[]{:S(2)}, u32[]{:S(2)}) collective-permute-start(bf16[4,944,128]{2,1,0:T(8,128)(2,1)S(1)} %bitcast.413), channel_id=1, source_target_pairs={{0,4},{1,5},{6,2},{7,3},{8,12},{9,13},{14,10},{15,11},{16,20},{17,... | collective-permute-start | bytes 2899976 | tf_op jit(solution)/shard_map/ppermute | solution.py:214
  85.0 17.3 %collective-permute-start.12 = (bf16[512,1024]{1,0:T(8,128)(2,1)}, bf16[512,1024]{1,0:T(8,128)(2,1)}, u32[]{:S(2)}, u32[]{:S(2)}) collective-permute-start(bf16[512,1024]{1,0:T(8,128)(2,1)} %convolution_convert_fusion.6), channel_id=1, source_target_pairs={{0,4},{1,5},{2,6},{3,7},{4,0},{5,1},{6,2},{7,3},{8,12},{9,13},{10,... | collective-permute-start | bytes 3145736 | tf_op jit(solution)/shard_map/ppermute | solution.py:237
  86.6 14.6 %collective-permute-start.22 = (bf16[256,1024]{1,0:T(8,128)(2,1)S(1)}, bf16[256,1024]{1,0:T(8,128)(2,1)}, u32[]{:S(2)}, u32[]{:S(2)}) collective-permute-start(bf16[256,1024]{1,0:T(8,128)(2,1)S(1)} %copy-done.26), channel_id=1, source_target_pairs={{0,1},{1,0},{2,3},{3,2},{4,5},{5,4},{6,7},{7,6},{8,9},{9,8},{10,11... | collective-permute-start | bytes 1572872 | tf_op jit(solution)/shard_map/ppermute | solution.py:232
  104.5 13.7 %collective-permute-start.13 = (bf16[256,1024]{1,0:T(8,128)(2,1)S(1)}, bf16[256,1024]{1,0:T(8,128)(2,1)S(1)}, u32[]{:S(2)}, u32[]{:S(2)}) collective-permute-start(bf16[256,1024]{1,0:T(8,128)(2,1)S(1)} %fusion.61), channel_id=1, source_target_pairs={{0,1},{1,0},{2,3},{3,2},{4,5},{5,4},{6,7},{7,6},{8,9},{9,8},{10,11... | collective-permute-start | bytes 1572872 | tf_op jit(solution)/shard_map/ppermute | solution.py:240
  105.9 13.9 %collective-permute-start.23 = (bf16[512,1024]{1,0:T(8,128)(2,1)}, bf16[512,1024]{1,0:T(8,128)(2,1)}, u32[]{:S(2)}, u32[]{:S(2)}) collective-permute-start(bf16[512,1024]{1,0:T(8,128)(2,1)} %pad_maximum_fusion.17), channel_id=1, source_target_pairs={{0,4},{1,5},{2,6},{3,7},{4,0},{5,1},{6,2},{7,3},{8,12},{9,13},{10,... | collective-permute-start | bytes 3145736 | tf_op jit(solution)/shard_map/ppermute | solution.py:233
  107.4 26.7 %collective-permute-start.19 = (bf16[4,2,128,688]{2,3,1,0:T(8,128)(2,1)}, bf16[4,2,128,688]{2,3,1,0:T(8,128)(2,1)}, u32[]{:S(2)}, u32[]{:S(2)}) collective-permute-start(bf16[4,2,128,688]{2,3,1,0:T(8,128)(2,1)} %bitcast.42), channel_id=1, source_target_pairs={{0,4},{1,5},{6,2},{7,3},{8,12},{9,13},{14,10},{15,11},{16,20},{17,... | collective-permute-start | bytes 4227080 | tf_op jit(solution)/shard_map/ppermute | solution.py:214
  119.5 13.1 %collective-permute-start.14 = (bf16[256,1024]{1,0:T(8,128)(2,1)}, bf16[256,1024]{1,0:T(8,128)(2,1)}, u32[]{:S(2)}, u32[]{:S(2)}) collective-permute-start(bf16[256,1024]{1,0:T(8,128)(2,1)} %multiply_convert_fusion.3), channel_id=1, source_target_pairs={{0,1},{1,0},{2,3},{3,2},{4,5},{5,4},{6,7},{7,6},{8,9},{9,8},{10,11... | collective-permute-start | bytes 1572872 | tf_op jit(solution)/shard_map/ppermute | solution.py:232
  184.9 28.2 %collective-permute-start.45 = (bf16[2,2,688,128]{3,2,1,0:T(8,128)(2,1)}, bf16[2,2,688,128]{3,2,1,0:T(8,128)(2,1)}, u32[]{:S(2)}, u32[]{:S(2)}) collective-permute-start(bf16[2,2,688,128]{3,2,1,0:T(8,128)(2,1)} %dynamic-slice_bitcast_fusion.1), channel_id=1, source_target_pairs={{0,8},{1,9},{2,10},{3,11},{4,20},{5,21},{6,22},{7,23},{8,0},{9,1},... | collective-permute-start | bytes 2113544 | tf_op jit(solution)/shard_map/ppermute | solution.py:250
  201.9 25.5 %collective-permute-start.20 = (bf16[512,1024]{1,0:T(8,128)(2,1)S(1)}, bf16[512,1024]{1,0:T(8,128)(2,1)S(1)}, u32[]{:S(2)}, u32[]{:S(2)}) collective-permute-start(bf16[512,1024]{1,0:T(8,128)(2,1)S(1)} %convolution_convert_fusion.5), channel_id=1, source_target_pairs={{0,4},{1,5},{2,6},{3,7},{4,0},{5,1},{6,2},{7,3},{8,12},{9,13},{10,... | collective-permute-start | bytes 3145736 | tf_op jit(solution)/shard_map/ppermute | solution.py:237
  211.8 37.1 %collective-permute-start.38 = (bf16[2,2,2,128,688]{3,4,2,1,0:T(8,128)(2,1)S(1)}, bf16[2,2,2,128,688]{3,4,2,1,0:T(8,128)(2,1)S(1)}, u32[]{:S(2)}, u32[]{:S(2)}) collective-permute-start(bf16[2,2,2,128,688]{3,4,2,1,0:T(8,128)(2,1)S(1)} %dynamic-slice_bitcast_fusion), channel_id=1, source_target_pairs={{0,8},{1,9},{2,10},{3,11},{4,20},{5,21},{6,22},{7,23},{8,0},{9,1},... | collective-permute-start | bytes 4227080 | tf_op jit(solution)/shard_map/ppermute | solution.py:250
  217.7 23.7 %collective-permute-start.25 = (bf16[256,1024]{1,0:T(8,128)(2,1)S(1)}, bf16[256,1024]{1,0:T(8,128)(2,1)S(1)}, u32[]{:S(2)}, u32[]{:S(2)}) collective-permute-start(bf16[256,1024]{1,0:T(8,128)(2,1)S(1)} %fusion.63), channel_id=1, source_target_pairs={{0,1},{1,0},{2,3},{3,2},{4,5},{5,4},{6,7},{7,6},{8,9},{9,8},{10,11... | collective-permute-start | bytes 1572872 | tf_op jit(solution)/shard_map/ppermute | solution.py:240
  226.1 13.8 %collective-permute-start.47 = (bf16[2,688,128]{2,1,0:T(8,128)(2,1)S(1)}, bf16[2,688,128]{2,1,0:T(8,128)(2,1)S(1)}, u32[]{:S(2)}, u32[]{:S(2)}) collective-permute-start(bf16[2,688,128]{2,1,0:T(8,128)(2,1)S(1)} %bitcast_convert_fusion.3), channel_id=1, source_target_pairs={{2,0},{3,1},{4,6},{5,7},{10,8},{11,9},{12,14},{13,15},{18,16},{19,... | collective-permute-start | bytes 1056776 | tf_op jit(solution)/shard_map/ppermute | solution.py:253
  228.5 17.8 %collective-permute-start.21 = (bf16[256,1024]{1,0:T(8,128)(2,1)S(1)}, bf16[256,1024]{1,0:T(8,128)(2,1)S(1)}, u32[]{:S(2)}, u32[]{:S(2)}) collective-permute-start(bf16[256,1024]{1,0:T(8,128)(2,1)S(1)} %fusion.62), channel_id=1, source_target_pairs={{0,1},{1,0},{2,3},{3,2},{4,5},{5,4},{6,7},{7,6},{8,9},{9,8},{10,11... | collective-permute-start | bytes 1572872 | tf_op jit(solution)/shard_map/ppermute | solution.py:240
  248.0 13.1 %collective-permute-start.26 = (bf16[256,1024]{1,0:T(8,128)(2,1)S(1)}, bf16[256,1024]{1,0:T(8,128)(2,1)S(1)}, u32[]{:S(2)}, u32[]{:S(2)}) collective-permute-start(bf16[256,1024]{1,0:T(8,128)(2,1)S(1)} %get-tuple-element.59), channel_id=1, source_target_pairs={{0,1},{1,0},{2,3},{3,2},{4,5},{5,4},{6,7},{7,6},{8,9},{9,8},{10,11... | collective-permute-start | bytes 1572872 | tf_op jit(solution)/shard_map/ppermute | solution.py:232
  249.3 15.5 %collective-permute-start.39 = (bf16[1,2,2,128,688]{3,4,2,1,0:T(8,128)(2,1)S(1)}, bf16[1,2,2,128,688]{3,4,2,1,0:T(8,128)(2,1)S(1)}, u32[]{:S(2)}, u32[]{:S(2)}) collective-permute-start(bf16[1,2,2,128,688]{3,4,2,1,0:T(8,128)(2,1)S(1)} %dynamic-slice_convert_fusion), channel_id=1, source_target_pairs={{0,16},{1,17},{2,18},{3,19},{4,12},{5,13},{6,14},{7,15},{8,24},{9,... | collective-permute-start | bytes 2113544 | tf_op jit(solution)/shard_map/ppermute | solution.py:250
  261.2 28.6 %collective-permute-start.27 = (bf16[512,1024]{1,0:T(8,128)(2,1)S(1)}, bf16[512,1024]{1,0:T(8,128)(2,1)S(1)}, u32[]{:S(2)}, u32[]{:S(2)}) collective-permute-start(bf16[512,1024]{1,0:T(8,128)(2,1)S(1)} %pad_maximum_fusion.18), channel_id=1, source_target_pairs={{0,4},{1,5},{2,6},{3,7},{4,0},{5,1},{6,2},{7,3},{8,12},{9,13},{10,... | collective-permute-start | bytes 3145736 | tf_op jit(solution)/shard_map/ppermute | solution.py:233
  265.0 21.5 %collective-permute-start.40 = (bf16[2,2,128,688]{2,3,1,0:T(8,128)(2,1)S(1)}, bf16[2,2,128,688]{2,3,1,0:T(8,128)(2,1)S(1)}, u32[]{:S(2)}, u32[]{:S(2)}) collective-permute-start(bf16[2,2,128,688]{2,3,1,0:T(8,128)(2,1)S(1)} %bitcast_convert_fusion.1), channel_id=1, source_target_pairs={{2,0},{3,1},{4,6},{5,7},{10,8},{11,9},{12,14},{13,15},{18,16},{19,... | collective-permute-start | bytes 2113544 | tf_op jit(solution)/shard_map/ppermute | solution.py:253
  267.3 56.7 %collective-permute-start.51 = (bf16[4,1,688,128]{3,2,0,1:T(8,128)(2,1)}, bf16[4,1,688,128]{3,2,0,1:T(8,128)(2,1)}, u32[]{:S(2)}, u32[]{:S(2)}) collective-permute-start(bf16[4,1,688,128]{3,2,0,1:T(8,128)(2,1)} %bitcast.125), channel_id=1, source_target_pairs={{0,4},{1,5},{2,6},{3,7},{4,0},{5,1},{6,2},{7,3},{8,12},{9,13},{10,... | collective-permute-start | bytes 2113544 | tf_op jit(solution)/shard_map/ppermute | solution.py:277
  287.5 27.7 %collective-permute-start.41 = (bf16[1,2,128,688]{2,3,1,0:T(8,128)(2,1)}, bf16[1,2,128,688]{2,3,1,0:T(8,128)(2,1)}, u32[]{:S(2)}, u32[]{:S(2)}) collective-permute-start(bf16[1,2,128,688]{2,3,1,0:T(8,128)(2,1)} %constant_dynamic-slice_fusion.1), channel_id=1, source_target_pairs={{0,4},{1,5},{6,2},{7,3},{8,12},{9,13},{14,10},{15,11},{16,20},{17,... | collective-permute-start | bytes 1056776 | tf_op jit(solution)/shard_map/ppermute | solution.py:260
  316.2 19.1 %collective-permute-start.31 = (bf16[2,2,128,1024]{3,2,1,0:T(8,128)(2,1)S(1)}, bf16[2,2,128,1024]{3,2,1,0:T(8,128)(2,1)S(1)}, u32[]{:S(2)}, u32[]{:S(2)}) collective-permute-start(bf16[2,2,128,1024]{3,2,1,0:T(8,128)(2,1)S(1)} %fusion.45), channel_id=1, source_target_pairs={{0,8},{1,9},{2,10},{3,11},{4,20},{5,21},{6,22},{7,23},{8,0},{9,1},... | collective-permute-start | bytes 3145736 | tf_op jit(solution)/shard_map/ppermute | solution.py:250
  318.6 25.7 %collective-permute-start.28 = (bf16[576,1024]{1,0:T(8,128)(2,1)S(1)}, bf16[576,1024]{1,0:T(8,128)(2,1)S(1)}, u32[]{:S(2)}, u32[]{:S(2)}) collective-permute-start(bf16[576,1024]{1,0:T(8,128)(2,1)S(1)} %convolution_convert_fusion.4), channel_id=1, source_target_pairs={{0,4},{1,5},{2,6},{3,7},{4,0},{5,1},{6,2},{7,3},{8,12},{9,13},{10,... | collective-permute-start | bytes 3538952 | tf_op jit(solution)/shard_map/ppermute | solution.py:377
  323.2 21.0 %collective-permute-start.43 = (bf16[2,1,2,128,688]{3,4,2,0,1:T(8,128)(2,1)S(1)}, bf16[2,1,2,128,688]{3,4,2,0,1:T(8,128)(2,1)S(1)}, u32[]{:S(2)}, u32[]{:S(2)}) collective-permute-start(bf16[2,1,2,128,688]{3,4,2,0,1:T(8,128)(2,1)S(1)} %fusion.65), channel_id=1, source_target_pairs={{0,8},{1,9},{2,18},{3,19},{4,20},{5,21},{6,14},{7,15},{8,0},{9,1},... | collective-permute-start | bytes 2113544 | tf_op jit(solution)/shard_map/ppermute | solution.py:192
  345.8 16.2 %collective-permute-start.29 = (bf16[320,1024]{1,0:T(8,128)(2,1)S(1)}, bf16[320,1024]{1,0:T(8,128)(2,1)S(1)}, u32[]{:S(2)}, u32[]{:S(2)}) collective-permute-start(bf16[320,1024]{1,0:T(8,128)(2,1)S(1)} %pad_maximum_fusion.26), channel_id=1, source_target_pairs={{0,1},{1,0},{2,3},{3,2},{4,5},{5,4},{6,7},{7,6},{8,9},{9,8},{10,11... | collective-permute-start | bytes 1966088 | tf_op jit(solution)/shard_map/ppermute | solution.py:381
  346.1 75.0 %collective-permute-start.44 = (bf16[4,1,2,128,688]{3,4,2,0,1:T(8,128)(2,1)S(1)}, bf16[4,1,2,128,688]{3,4,2,0,1:T(8,128)(2,1)}, u32[]{:S(2)}, u32[]{:S(2)}) collective-permute-start(bf16[4,1,2,128,688]{3,4,2,0,1:T(8,128)(2,1)S(1)} %bitcast.400), channel_id=1, source_target_pairs={{0,4},{1,5},{2,6},{3,7},{4,0},{5,1},{6,2},{7,3},{8,12},{9,13},{10,... | collective-permute-start | bytes 4227080 | tf_op jit(solution)/shard_map/ppermute | solution.py:277
  346.4 18.9 %collective-permute-start.33 = (bf16[2,128,1024]{2,1,0:T(8,128)(2,1)S(1)}, bf16[2,128,1024]{2,1,0:T(8,128)(2,1)S(1)}, u32[]{:S(2)}, u32[]{:S(2)}) collective-permute-start(bf16[2,128,1024]{2,1,0:T(8,128)(2,1)S(1)} %bitcast_convert_fusion.2), channel_id=1, source_target_pairs={{2,0},{3,1},{4,6},{5,7},{10,8},{11,9},{12,14},{13,15},{18,16},{19,... | collective-permute-start | bytes 1572872 | tf_op jit(solution)/shard_map/ppermute | solution.py:253
  366.2 45.3 %collective-permute-start.34 = (bf16[1,128,1024]{2,1,0:T(8,128)(2,1)}, bf16[1,128,1024]{2,1,0:T(8,128)(2,1)}, u32[]{:S(2)}, u32[]{:S(2)}) collective-permute-start(bf16[1,128,1024]{2,1,0:T(8,128)(2,1)} %constant_dynamic-slice_fusion.2), channel_id=1, source_target_pairs={{0,4},{1,5},{6,2},{7,3},{8,12},{9,13},{14,10},{15,11},{16,20},{17,... | collective-permute-start | bytes 786440 | tf_op jit(solution)/shard_map/ppermute | solution.py:260
  (69 other events, 465.0 us)
